TPU v7x, 512 devices: a whole 4x8x8 slice. The times are simulated.
512 devices in a mesh: seq: 64 (over x, y, core), chan: 8 (over z).
Axes of the slice: x: 4, y: 8, z: 8, core: 2. Of those that a mesh axis runs over, the one named last changes fastest.
Arguments:
- gate_outer: bfloat16 [8192, 4096], P('seq', 'chan'), may hold values from -520 to 520
- gate_inner: bfloat16 [8192, 4096], P('seq', 'chan'), may hold values from -6 to 6
- value_in: bfloat16 [8192, 4096], P('seq', 'chan'), may hold values from -6 to 6
- pole_rates: float32 [8, 4096], P(None, 'chan'), may hold values from 0 to 1, as said below
- pole_weights: float32 [8, 4096], P(None, 'chan'), may hold values from -4 to 4
- skip_gain: float32 [4096], P('chan'), may hold values from -1 to 1
- query_rows: bfloat16 [8192, 4096], P('seq', 'chan'), may hold values from -6 to 6
- key_rows: bfloat16 [8192, 4096], P('seq', 'chan'), may hold values from -6 to 6
Outputs:
- mixed: bfloat16 [8192, 4096], P('seq', 'chan')
Inputs may be any that keep to these rules, and one draw needn't show every extreme that they name: `pole_rates`: each rate is positive and at most 1/30.
All inputs are finite; a program needn't handle non-finite values.
Results may differ from a plain program's by a relative error of at most 0.0065.
Values may be sent and summed in bfloat16 or wider, within the bound.
A program may use at most 128 MiB of HBM per device.

v0:
```python
import math
import jax
import jax.numpy as jnp
from jax import lax
from jax.sharding import PartitionSpec as P

HD = 128


def prefix(part, axis, combine, identity):
    place = lax.axis_index(axis)
    gathered = jax.tree.map(lambda a: lax.all_gather(a, axis), part)
    state = jax.tree.map(lambda a, e: jnp.zeros_like(a) + jnp.asarray(e, a.dtype), part, identity)

    def one(turn, state):
        return combine(
            state, jax.tree.map(lambda a: lax.dynamic_index_in_dim(a, turn, 0, False), gathered)
        )

    return lax.fori_loop(0, place, one, state)


def block_update(carried, queries, query_pos, key_part, value_part, key_start, score_scale):
    run_max, run_sum, run_acc = carried
    heads_here = run_max.shape[0]
    key_count = key_part.shape[0]
    query_heads = queries.reshape(queries.shape[0], heads_here, -1)
    key_heads = key_part.reshape(key_count, heads_here, -1)
    value_heads = value_part.reshape(key_count, heads_here, -1)
    scores = (
        jnp.einsum("qhd,khd->hqk", query_heads, key_heads, preferred_element_type=jnp.float32)
        * score_scale
    )
    key_pos = key_start + jnp.arange(key_count, dtype=jnp.int32)
    visible = key_pos[None, None, :] <= query_pos[None, :, None]
    scores = jnp.where(visible, scores, -1e30)
    new_max = jnp.maximum(run_max, jnp.max(scores, axis=2))
    rescale = jnp.exp(run_max - new_max)
    expo = jnp.where(visible, jnp.exp(scores - new_max[:, :, None]), 0.0)
    new_sum = run_sum * rescale + jnp.sum(expo, axis=2)
    new_acc = run_acc * rescale[:, :, None] + jnp.einsum(
        "hqk,khd->hqd", expo.astype(jnp.bfloat16), value_heads, preferred_element_type=jnp.float32
    )
    return (new_max, new_sum, new_acc)


def fold_keys(carried, queries, query_pos, pieces, score_scale):
    key_piece, value_piece = pieces
    count_rows = key_piece.shape[0]
    step_rows = math.gcd(count_rows, 1024)

    def one_step(step_index, current):
        sub_start = step_index * step_rows
        key_part = lax.dynamic_slice_in_dim(key_piece, sub_start, step_rows, 0)
        value_part = lax.dynamic_slice_in_dim(value_piece, sub_start, step_rows, 0)
        return block_update(
            current, queries, query_pos, key_part, value_part, sub_start, score_scale
        )

    return lax.fori_loop(0, count_rows // step_rows, one_step, carried)


def finish(carried):
    run_max, run_sum, run_acc = carried
    normed = run_acc / run_sum[:, :, None]
    heads_here, rows_here, depth = normed.shape
    return (
        jnp.transpose(normed, (1, 0, 2)).reshape(rows_here, heads_here * depth).astype(jnp.bfloat16)
    )


def local(
    gate_outer, gate_inner, value_in, pole_rates, pole_weights, skip_gain, query_rows, key_rows
):
    tok_rows, width = gate_outer.shape
    poles_here = pole_rates.shape[0]
    seq_index = lax.axis_index("seq")
    chan_count = lax.axis_size("chan")
    gated = gate_inner.astype(jnp.float32) * value_in.astype(jnp.float32)
    offsets = jnp.arange(tok_rows, dtype=jnp.float32)
    growth = jnp.exp(offsets[:, None, None] * pole_rates[None, :, :])
    weighted = growth * gated[:, None, :]
    lower = (jnp.arange(tok_rows)[:, None] >= jnp.arange(tok_rows)[None, :]).astype(jnp.float32)
    running = jnp.dot(
        lower, weighted.reshape(tok_rows, poles_here * width), precision=lax.Precision.HIGHEST
    )
    running = running.reshape(tok_rows, poles_here, width)
    block_span = jnp.float32(tok_rows)
    summary = running[-1] * jnp.exp(-(block_span - 1.0) * pole_rates)

    def chain_states(earlier, later):
        fade = jnp.exp(-block_span * later[1] * pole_rates)
        return (later[0] + fade * earlier[0], earlier[1] + later[1])

    identity = (jnp.zeros_like(summary), jnp.zeros((1, 1), jnp.float32))
    carry_in, block_count = prefix(
        (summary, jnp.ones((1, 1), jnp.float32)), "seq", chain_states, identity
    )
    decayed = jnp.exp(-offsets[:, None, None] * pole_rates[None, :, :])
    modal = decayed * (running + (jnp.exp(-pole_rates) * carry_in)[None, :, :])
    filtered = jnp.sum(modal * (pole_weights * jnp.sqrt(pole_rates))[None, :, :], axis=1)
    conv_out = gate_outer.astype(jnp.float32) * (filtered + skip_gain[None, :] * gated)
    local_squares = jnp.sum(conv_out * conv_out, axis=1)
    total_squares = lax.psum(local_squares, "chan")
    mean_square = total_squares / (width * chan_count)
    values = (conv_out * lax.rsqrt(mean_square[:, None] + 1e-06)).astype(jnp.bfloat16)
    score_scale = HD ** (-0.5)
    heads_here = width // HD
    my_start = seq_index * tok_rows
    all_pos = my_start + jnp.arange(tok_rows, dtype=jnp.int32)
    final_state = fold_keys(
        (
            jnp.full((heads_here, tok_rows), -1e30, jnp.float32),
            jnp.zeros((heads_here, tok_rows), jnp.float32),
            jnp.zeros((heads_here, tok_rows, HD), jnp.float32),
        ),
        query_rows,
        all_pos,
        (
            lax.all_gather(key_rows, "seq", axis=0, tiled=True),
            lax.all_gather(values, "seq", axis=0, tiled=True),
        ),
        score_scale,
    )
    mixed = finish(final_state)
    return mixed


def solution(mesh):
    in_specs = (
        P("seq", "chan"),
        P("seq", "chan"),
        P("seq", "chan"),
        P(None, "chan"),
        P(None, "chan"),
        P("chan"),
        P("seq", "chan"),
        P("seq", "chan"),
    )
    out_specs = P("seq", "chan")
    return jax.shard_map(local, mesh=mesh, in_specs=in_specs, out_specs=out_specs, check_vma=False)
```

profile of v0, /device:TPU:1, one launch (start us, length us, event | category | flops | bytes accessed | tf_op | source)
XLA Modules:
  0.0 426.7 jit_solution(17308309685470993890)
XLA Ops:
  6.5 0.7 copy.35
  7.3 1.0 convert_multiply_fusion
  8.5 1.6 copy.36
  10.2 1.6 fusion.21
  11.8 0.6 exponential_multiply_fusion
  12.5 0.8 copy.26
  13.4 3.0 copy.37
  16.4 1.3 dynamic-slice
  17.7 0.7 dynamic-update-slice
  18.5 130.3 %all-reduce = f32[64]{0:T(128)S(1)} all-reduce(f32[64]{0:T(128)S(1)} %dynamic-update-slice), channel_id=1, replica_groups=mesh['seq'=64,'chan'=8] {'seq'}, use_global_device_ids=true, to_apply=%add | all-reduce | flops 64 | bytes 512
  148.8 2.0 while.30
  148.9 0.6 fusion.41
  149.5 1.4 bitcast_add_fusion.3
  150.9 2.6 fusion.20
  153.7 16.0 %psum.7 = f32[128]{0:T(128)S(1)} all-reduce(f32[128]{0:T(128)S(1)} %multiply_reduce_fusion), channel_id=1, replica_groups=mesh['seq'=64,'chan'=8] {'chan'}, use_global_device_ids=true, to_apply=%region_4.5 | all-reduce | flops 128 | bytes 1024 | tf_op jit(solution)/shard_map/psum | solution.py:104
  169.7 0.7 multiply_convert_fusion
  170.5 21.5 %all-gather.5.cloned.1.call-done = bf16[8192,512]{0,1:T(8,128)(2,1)} async-done(((bf16[128,512]{0,1:T(8,128)(2,1)}), bf16[8192,512]{0,1:T(8,128)(2,1)}) %all-gather.5.cloned.1.call-update) | async-done | bytes 8388624 | tf_op jit(solution)/shard_map/all_gather | solution.py:120
  192.0 183.1 %all-gather.7.cloned.1.call-done = bf16[8192,512]{1,0:T(8,128)(2,1)} async-done(((bf16[128,512]{1,0:T(8,128)(2,1)}), bf16[8192,512]{1,0:T(8,128)(2,1)}) %all-gather.7.cloned.1.call-update) | async-done | bytes 8388624 | tf_op jit(solution)/shard_map/all_gather | solution.py:121
  375.1 44.3 %while.31 = (s32[]{:T(128)}, f32[4,128]{1,0:T(4,128)S(1)}, f32[4,128]{1,0:T(4,128)S(1)}, f32[4,128,128]{2,1,0:T(8,128)S(1)}, bf16[8192,512]{0,1:T(8,128)(2,1)}, ...) while((s32[]{:T(128)}, f32[4,128]{1,0:T(4,128)S(1)}, ...), condition=%wide.region_8.9_spmd.clone, body=%wide.region_5.8_spmd.clone.sunk | while | flops 275582592 | bytes 15901895 | solution.py:60
  375.3 1.3 constant_dynamic-slice_fusion.6
  376.6 0.5 copy.48
  377.2 1.3 constant_dynamic-slice_fusion.5
  378.5 0.6 fusion.46
  379.7 0.9 convolution_add_fusion.2
  380.9 1.3 constant_dynamic-slice_fusion.6
  382.2 0.5 copy.48
  382.7 1.3 constant_dynamic-slice_fusion.5
  384.0 0.6 fusion.46
  384.7 0.5 fusion.47
  385.2 0.9 convolution_add_fusion.2
  386.4 1.3 constant_dynamic-slice_fusion.6
  387.7 0.5 copy.48
  388.2 1.3 constant_dynamic-slice_fusion.5
  389.5 0.6 fusion.46
  390.2 0.5 fusion.47
  390.7 0.9 convolution_add_fusion.2
  391.9 1.3 constant_dynamic-slice_fusion.6
  393.2 0.5 copy.48
  393.8 1.3 constant_dynamic-slice_fusion.5
  395.1 0.6 fusion.46
  396.3 0.9 convolution_add_fusion.2
  397.5 1.3 constant_dynamic-slice_fusion.6
  398.8 0.5 copy.48
  399.3 1.3 constant_dynamic-slice_fusion.5
  400.6 0.6 fusion.46
  401.3 0.5 fusion.47
  401.8 0.9 convolution_add_fusion.2
  403.0 1.3 constant_dynamic-slice_fusion.6
  404.3 0.5 copy.48
  404.9 1.3 constant_dynamic-slice_fusion.5
  406.2 0.6 fusion.46
  406.8 0.5 fusion.47
  407.4 0.9 convolution_add_fusion.2
  408.5 1.3 constant_dynamic-slice_fusion.6
  409.8 0.5 copy.48
  410.4 1.3 constant_dynamic-slice_fusion.5
  411.7 0.6 fusion.46
  412.9 0.9 convolution_add_fusion.2
  414.1 1.3 constant_dynamic-slice_fusion.6
  415.4 0.5 copy.48
  415.9 1.3 constant_dynamic-slice_fusion.5
  417.2 0.6 fusion.46
  418.4 0.9 convolution_add_fusion.2
  419.4 0.8 copy_bitcast_fusion
  (87 shorter events, 4.8 us)
Async XLA Ops:
  6.5 142.3 %all-gather.9.cloned.1.call-start = ((), (), s32[]{:S(2)}) async-start(), calls=%async_computation.2 | async-start | bytes 1064960 | tf_op jit(solution)/shard_map/all_gather | solution.py:12
  10.2 1.7 copy-start.1
  10.2 2.3 copy-start.5
  12.5 179.6 %all-gather.5.cloned.1.call-start = ((), (), s32[]{:S(2)}) async-start(), calls=%async_computation | async-start | bytes 8519680 | tf_op jit(solution)/shard_map/all_gather | solution.py:120
  13.3 361.8 %all-gather.7.cloned.1.call-start = ((), (), s32[]{:S(2)}) async-start(), calls=%async_computation.1 | async-start | bytes 8519680 | tf_op jit(solution)/shard_map/all_gather | solution.py:121
  13.4 137.5 %copy-start.6 = (f32[8,512]{1,0:T(8,128)S(1)}, f32[8,512]{1,0:T(8,128)}, u32[]{:S(2)}) copy-start(f32[8,512]{1,0:T(8,128)} %param.16) | copy-start | bytes 49156
  16.4 137.1 %copy-start.2 = (bf16[128,512]{1,0:T(8,128)(2,1)S(1)}, bf16[128,512]{1,0:T(8,128)(2,1)}, u32[]{:S(2)}) copy-start(bf16[128,512]{1,0:T(8,128)(2,1)} %param.14) | copy-start | bytes 393220
  16.4 137.1 %copy-start.3 = (bf16[128,512]{1,0:T(8,128)(2,1)S(1)}, bf16[128,512]{1,0:T(8,128)(2,1)}, u32[]{:S(2)}) copy-start(bf16[128,512]{1,0:T(8,128)(2,1)} %param.13) | copy-start | bytes 393220
  16.4 137.1 %copy-start.4 = (bf16[128,512]{1,0:T(8,128)(2,1)S(1)}, bf16[128,512]{1,0:T(8,128)(2,1)}, u32[]{:S(2)}) copy-start(bf16[128,512]{1,0:T(8,128)(2,1)} %param.12) | copy-start | bytes 393220
  16.4 137.1 %copy-start.7 = (f32[512]{0:T(512)S(1)}, f32[512]{0:T(512)}, u32[]{:S(2)}) copy-start(f32[512]{0:T(512)} %param.17) | copy-start | bytes 6148
  150.9 224.2 %copy-start = (bf16[128,512]{1,0:T(8,128)(2,1)S(1)}, bf16[128,512]{1,0:T(8,128)(2,1)}, u32[]{:S(2)}) copy-start(bf16[128,512]{1,0:T(8,128)(2,1)} %param.18) | copy-start | bytes 393220
Sparse Core Ops, SparseCore 0:
  12.6 87.8 all-gather.8
  103.6 88.3 all-gather.4
  195.4 179.6 all-gather.6
where the time goes:
time: 433 us; the launch traced here: 427 us
  waiting for transfers between devices  205 us (47%)
  blocking collectives  146 us (34%)
  local copies, waits for them, and re-layouts  33.7 us (8%)
  other arithmetic  14.1 us (3%)
  matrix products  13.9 us (3%)
  between operations  13.3 us (3%)
    all_gather x1, waiting for transfers between devices, local(): lax.all_gather(values, 'seq', axis=0, tiled=True)  183 us
    unnamed x1, blocking collectives  130 us
    all_gather x1, waiting for transfers between devices, local(): lax.all_gather(key_rows, 'seq', axis=0, tiled=True)  21.5 us
    psum x1, blocking collectives, local(): total_squares = lax.psum(local_squares, 'chan')  16 us
    dynamic_slice x16, local copies, waits for them, and re-layouts, one_step(): value_part = lax.dynamic_slice_in_dim(value_piece, sub_start, step_rows, 0)  14.7 us
    dynamic_slice x8, local copies, waits for them, and re-layouts, one_step(): key_part = lax.dynamic_slice_in_dim(key_piece, sub_start, step_rows, 0)  10.4 us
  transfers between devices with their start and end apart: 3, of which 2 were waited for; matrix products, arithmetic and copies ran while one was open for 3% of the time, Pallas kernels for 0%

commit v1 on v0

--- a/solution.py
+++ b/solution.py
@@ -101,7 +101,7 @@
     filtered = jnp.sum(modal * (pole_weights * jnp.sqrt(pole_rates))[None, :, :], axis=1)
     conv_out = gate_outer.astype(jnp.float32) * (filtered + skip_gain[None, :] * gated)
     local_squares = jnp.sum(conv_out * conv_out, axis=1)
-    total_squares = lax.psum(local_squares, "chan")
+    total_squares = jnp.sum(lax.all_gather(local_squares, "chan"), axis=0)
     mean_square = total_squares / (width * chan_count)
     values = (conv_out * lax.rsqrt(mean_square[:, None] + 1e-06)).astype(jnp.bfloat16)
     score_scale = HD ** (-0.5)

time: 433 us -> 433 us (level)
    psum x1 -> x0, blocking collectives: 16 us -> none  [local(): total_squares = lax.psum(local_squares, 'chan')]
    all_gather x0 -> x1, blocking collectives: none -> 15.1 us  [local(): total_squares = jnp.sum(lax.all_gather(local_squares, 'chan'), axis=0)]
where the time goes in v1:
time: 433 us; the launch traced here: 426 us
  waiting for transfers between devices  205 us (47%)
  blocking collectives  145 us (33%)
  local copies, waits for them, and re-layouts  33.7 us (8%)
  other arithmetic  14.1 us (3%)
  matrix products  13.9 us (3%)
  between operations  13.3 us (3%)
    all_gather x1, waiting for transfers between devices, local(): lax.all_gather(values, 'seq', axis=0, tiled=True)  182 us
    unnamed x1, blocking collectives  130 us
    all_gather x1, waiting for transfers between devices, local(): lax.all_gather(key_rows, 'seq', axis=0, tiled=True)  22.6 us
    all_gather x1, blocking collectives, local(): total_squares = jnp.sum(lax.all_gather(local_squares, 'chan'), axis=0)  15.1 us
    dynamic_slice x16, local copies, waits for them, and re-layouts, one_step(): value_part = lax.dynamic_slice_in_dim(value_piece, sub_start, step_rows, 0)  14.7 us
    dynamic_slice x8, local copies, waits for them, and re-layouts, one_step(): key_part = lax.dynamic_slice_in_dim(key_piece, sub_start, step_rows, 0)  10.4 us
  transfers between devices with their start and end apart: 3, of which 2 were waited for; matrix products, arithmetic and copies ran while one was open for 3% of the time, Pallas kernels for 0%

profile of v1, /device:TPU:1, one launch (start us, length us, event | category | flops | bytes accessed | tf_op | source)
XLA Modules:
  0.0 425.9 jit_solution(10612231366201208313)
XLA Ops:
  6.5 0.7 copy.35
  7.3 1.0 convert_multiply_fusion
  8.5 1.6 copy.36
  10.2 1.6 fusion.21
  11.8 0.6 exponential_multiply_fusion
  12.5 0.8 copy.26
  13.4 3.0 copy.37
  16.4 1.3 dynamic-slice
  17.7 0.7 dynamic-update-slice
  18.5 130.3 %all-reduce = f32[64]{0:T(128)S(1)} all-reduce(f32[64]{0:T(128)S(1)} %dynamic-update-slice), channel_id=1, replica_groups=mesh['seq'=64,'chan'=8] {'seq'}, use_global_device_ids=true, to_apply=%add | all-reduce | flops 64 | bytes 512
  148.8 2.0 while.30
  148.9 0.6 fusion.41
  149.5 1.4 bitcast_add_fusion.3
  150.9 2.6 fusion.20
  153.7 15.1 %all-gather.2 = f32[8,1,128]{2,1,0:T(1,128)S(1)} all-gather(f32[1,1,128]{2,1,0:T(1,128)S(1)} %bitcast.80), channel_id=3, replica_groups=mesh['seq'=64,'chan'=8] {'chan'}, dimensions={0}, use_global_device_ids=true | all-gather | bytes 4608 | tf_op jit(solution)/shard_map/all_gather | solution.py:104
  168.8 0.7 multiply_convert_fusion
  169.6 22.6 %all-gather.7.cloned.1.call-done = bf16[8192,512]{0,1:T(8,128)(2,1)} async-done(((bf16[128,512]{0,1:T(8,128)(2,1)}), bf16[8192,512]{0,1:T(8,128)(2,1)}) %all-gather.7.cloned.1.call-update) | async-done | bytes 8388624 | tf_op jit(solution)/shard_map/all_gather | solution.py:120
  192.2 182.0 %all-gather.9.cloned.1.call-done = bf16[8192,512]{1,0:T(8,128)(2,1)} async-done(((bf16[128,512]{1,0:T(8,128)(2,1)}), bf16[8192,512]{1,0:T(8,128)(2,1)}) %all-gather.9.cloned.1.call-update) | async-done | bytes 8388624 | tf_op jit(solution)/shard_map/all_gather | solution.py:121
  374.3 44.3 %while.31 = (s32[]{:T(128)}, f32[4,128]{1,0:T(4,128)S(1)}, f32[4,128]{1,0:T(4,128)S(1)}, f32[4,128,128]{2,1,0:T(8,128)S(1)}, bf16[8192,512]{0,1:T(8,128)(2,1)}, ...) while((s32[]{:T(128)}, f32[4,128]{1,0:T(4,128)S(1)}, ...), condition=%wide.region_8.9_spmd.clone, body=%wide.region_5.8_spmd.clone.sunk | while | flops 275582592 | bytes 15901895 | solution.py:60
  374.5 1.3 constant_dynamic-slice_fusion.6
  375.8 0.5 copy.48
  376.3 1.3 constant_dynamic-slice_fusion.5
  377.6 0.6 fusion.46
  378.3 0.5 fusion.47
  378.8 0.9 convolution_add_fusion.2
  380.0 1.3 constant_dynamic-slice_fusion.6
  381.3 0.5 copy.48
  381.9 1.3 constant_dynamic-slice_fusion.5
  383.2 0.6 fusion.46
  383.8 0.5 fusion.47
  384.4 0.9 convolution_add_fusion.2
  385.6 1.3 constant_dynamic-slice_fusion.6
  386.9 0.5 copy.48
  387.4 1.3 constant_dynamic-slice_fusion.5
  388.7 0.6 fusion.46
  389.9 0.9 convolution_add_fusion.2
  391.1 1.3 constant_dynamic-slice_fusion.6
  392.4 0.5 copy.48
  392.9 1.3 constant_dynamic-slice_fusion.5
  394.3 0.6 fusion.46
  394.9 0.5 fusion.47
  395.4 0.9 convolution_add_fusion.2
  396.6 1.3 constant_dynamic-slice_fusion.6
  397.9 0.5 copy.48
  398.5 1.3 constant_dynamic-slice_fusion.5
  399.8 0.6 fusion.46
  400.4 0.5 fusion.47
  401.0 0.9 convolution_add_fusion.2
  402.2 1.3 constant_dynamic-slice_fusion.6
  403.5 0.5 copy.48
  404.0 1.3 constant_dynamic-slice_fusion.5
  405.3 0.6 fusion.46
  406.5 0.9 convolution_add_fusion.2
  407.7 1.3 constant_dynamic-slice_fusion.6
  409.0 0.5 copy.48
  409.6 1.3 constant_dynamic-slice_fusion.5
  410.9 0.6 fusion.46
  412.1 0.9 convolution_add_fusion.2
  413.2 1.3 constant_dynamic-slice_fusion.6
  414.6 0.5 copy.48
  415.1 1.3 constant_dynamic-slice_fusion.5
  416.4 0.6 fusion.46
  417.6 0.9 convolution_add_fusion.2
  418.5 0.8 copy_bitcast_fusion
  (88 shorter events, 4.8 us)
Async XLA Ops:
  6.5 142.3 %all-gather.11.cloned.1.call-start = ((), (), s32[]{:S(2)}) async-start(), calls=%async_computation.2 | async-start | bytes 1064960 | tf_op jit(solution)/shard_map/all_gather | solution.py:12
  10.2 1.7 copy-start.1
  10.2 2.3 copy-start.5
  12.5 179.7 %all-gather.7.cloned.1.call-start = ((), (), s32[]{:S(2)}) async-start(), calls=%async_computation | async-start | bytes 8519680 | tf_op jit(solution)/shard_map/all_gather | solution.py:120
  13.3 360.9 %all-gather.9.cloned.1.call-start = ((), (), s32[]{:S(2)}) async-start(), calls=%async_computation.1 | async-start | bytes 8519680 | tf_op jit(solution)/shard_map/all_gather | solution.py:121
  13.4 137.5 %copy-start.6 = (f32[8,512]{1,0:T(8,128)S(1)}, f32[8,512]{1,0:T(8,128)}, u32[]{:S(2)}) copy-start(f32[8,512]{1,0:T(8,128)} %param.16) | copy-start | bytes 49156
  16.4 137.1 %copy-start.2 = (bf16[128,512]{1,0:T(8,128)(2,1)S(1)}, bf16[128,512]{1,0:T(8,128)(2,1)}, u32[]{:S(2)}) copy-start(bf16[128,512]{1,0:T(8,128)(2,1)} %param.14) | copy-start | bytes 393220
  16.4 137.1 %copy-start.3 = (bf16[128,512]{1,0:T(8,128)(2,1)S(1)}, bf16[128,512]{1,0:T(8,128)(2,1)}, u32[]{:S(2)}) copy-start(bf16[128,512]{1,0:T(8,128)(2,1)} %param.13) | copy-start | bytes 393220
  16.4 137.1 %copy-start.4 = (bf16[128,512]{1,0:T(8,128)(2,1)S(1)}, bf16[128,512]{1,0:T(8,128)(2,1)}, u32[]{:S(2)}) copy-start(bf16[128,512]{1,0:T(8,128)(2,1)} %param.12) | copy-start | bytes 393220
  16.4 137.1 %copy-start.7 = (f32[512]{0:T(512)S(1)}, f32[512]{0:T(512)}, u32[]{:S(2)}) copy-start(f32[512]{0:T(512)} %param.17) | copy-start | bytes 6148
  150.9 223.4 %copy-start = (bf16[128,512]{1,0:T(8,128)(2,1)S(1)}, bf16[128,512]{1,0:T(8,128)(2,1)}, u32[]{:S(2)}) copy-start(bf16[128,512]{1,0:T(8,128)(2,1)} %param.18) | copy-start | bytes 393220
Sparse Core Ops, SparseCore 0:
  12.6 87.8 all-gather.10
  103.6 88.5 all-gather.6
  195.6 178.6 all-gather.8
